TPU v7x, 32 devices: a whole 2x2x4 slice. The times are simulated.
32 devices in a mesh: fsdp: 4 (over x, core), ctx: 4 (over z), tp: 2 (over y).
Axes of the slice: x: 2, y: 2, z: 4, core: 2. Of those that a mesh axis runs over, the one named last changes fastest.
Arguments:
- tokens: bfloat16 [8, 4096, 768], P('fsdp', 'ctx'), may hold values from -6 to 6
- qkv_weight: bfloat16 [768, 3, 768], P(('fsdp', 'ctx'), None, 'tp'), may hold values from -0.21875 to 0.21875
- qv_bias: bfloat16 [2, 768], P(None, 'tp'), may hold values from -3 to 3
- out_weight: bfloat16 [768, 768], P(('fsdp', 'ctx'), 'tp'), may hold values from -8 to 8
- up_weight: bfloat16 [768, 3072], P(('fsdp', 'ctx'), 'tp'), may hold values from -0.21875 to 0.21875
- up_bias: bfloat16 [3072], P('tp'), may hold values from -3 to 3
- down_weight: bfloat16 [768, 3072], P(('fsdp', 'ctx'), 'tp'), may hold values from -0.109375 to 0.109375
- norm_gains: bfloat16 [768, 2], P(('fsdp', 'ctx')), may hold values from 0.5 to 1.5
- row_biases: bfloat16 [768, 4], P(('fsdp', 'ctx')), may hold values from -3 to 3
- cotangent: bfloat16 [8, 4096, 768], P('fsdp', 'ctx'), may hold values from -6 to 6
Outputs:
- output: bfloat16 [8, 4096, 768], P('fsdp', ('ctx', 'tp'))
- tokens_grad: bfloat16 [8, 4096, 768], P('fsdp', ('ctx', 'tp'))
- qkv_weight_grad: float32 [768, 3, 768], P(('fsdp', 'ctx'), None, 'tp')
- qv_bias_grad: float32 [2, 768], P(None, 'tp')
- out_weight_grad: float32 [768, 768], P(('fsdp', 'ctx'), 'tp')
- up_weight_grad: float32 [768, 3072], P(('fsdp', 'ctx'), 'tp')
- up_bias_grad: float32 [3072], P('tp')
- down_weight_grad: float32 [768, 3072], P(('fsdp', 'ctx'), 'tp')
- norm_gains_grad: float32 [768, 2], P(('fsdp', 'ctx'))
- row_biases_grad: float32 [768, 4], P(('fsdp', 'ctx'))
All inputs are finite; a program needn't handle non-finite values.
Results may differ from a plain program's by a relative error of at most 0.02.
Values may be sent and summed in bfloat16 or wider, within the bound.
No kernel may reach another device: no remote copies, remote signals or barrier semaphores. Data moves between devices by JAX's collectives and lax.ppermute only.
A program may use at most 256 MiB of HBM per device.

v0:
```python
import jax
import jax.numpy as jnp
from jax import lax
from jax.sharding import PartitionSpec as P

HD = 64
epsilon = 1e-12
score_scale = 0.125
highest = lax.Precision.HIGHEST


def contract_last(left, right):
    return lax.dot_general(
        left, right, (((1,), (1,)), ((), ())), preferred_element_type=jnp.float32
    )


def contract_first(left, right):
    return lax.dot_general(
        left, right, (((0,), (0,)), ((), ())), preferred_element_type=jnp.float32
    )


def norm_forward(hidden, gain, shift):
    center = hidden - jnp.mean(hidden, axis=-1, keepdims=True)
    inv_scale = lax.rsqrt(jnp.mean(center * center, axis=-1, keepdims=True) + epsilon)
    normed = center * inv_scale
    return (normed * gain + shift, normed, inv_scale)


def norm_backward(grad_out, normed, inv_scale, gain):
    grad_norm = grad_out * gain
    return inv_scale * (
        grad_norm
        - jnp.mean(grad_norm, axis=-1, keepdims=True)
        - normed * jnp.mean(grad_norm * normed, axis=-1, keepdims=True)
    )


def gelu_exact(values):
    return jax.nn.gelu(values, approximate=False)


def split_heads(array, first_row, row_count, head_count):
    piece = lax.dynamic_slice_in_dim(array, first_row, row_count, 1)
    return piece.reshape(piece.shape[0], row_count, head_count, piece.shape[2] // head_count)


def block_scores(query_four, key_four):
    return (
        jnp.einsum("sqhd,skhd->shqk", query_four, key_four, preferred_element_type=jnp.float32)
        * score_scale
    )


def softmax_rows(scores, row_max, row_total):
    return jnp.exp(scores - row_max[..., None]) / row_total[..., None]


def score_grads(scores, row_max, row_total, row_delta, grad_four, value_four):
    prob_full = softmax_rows(scores, row_max, row_total)
    prob_grad = jnp.einsum(
        "sqhd,skhd->shqk", grad_four, value_four, preferred_element_type=jnp.float32
    )
    score_low = (prob_full * (prob_grad - row_delta[..., None])).astype(jnp.bfloat16)
    return (prob_full.astype(jnp.bfloat16), score_low)


def body(
    tokens,
    qkv_weight,
    qv_bias,
    out_weight,
    up_weight,
    up_bias,
    down_weight,
    norm_gains,
    row_biases,
    cotangent,
):
    seq_count, local_len, width = tokens.shape
    row_count = seq_count * local_len
    tp_count = lax.axis_size("tp")
    share_len = local_len // tp_count
    share_start = lax.axis_index("tp") * share_len

    def own_rows(array_three):
        return lax.dynamic_slice_in_dim(array_three, share_start, share_len, 1)

    def to_three(array_two):
        return array_two.reshape(seq_count, array_two.shape[0] // seq_count, array_two.shape[1])

    gathered = (
        lax.all_gather(qkv_weight, ("fsdp", "ctx"), axis=0, tiled=True),
        lax.all_gather(out_weight, ("fsdp", "ctx"), axis=0, tiled=True),
        lax.all_gather(up_weight, ("fsdp", "ctx"), axis=0, tiled=True),
        lax.all_gather(down_weight, ("fsdp", "ctx"), axis=0, tiled=True),
        lax.all_gather(norm_gains, ("fsdp", "ctx"), axis=0, tiled=True),
        lax.all_gather(row_biases, ("fsdp", "ctx"), axis=0, tiled=True),
    )
    w_qkv, w_out, w_up, w_down, gains_all, biases_all = gathered
    gains_f = gains_all.astype(jnp.float32)
    biases_f = biases_all.astype(jnp.float32)
    head_width = w_qkv.shape[2]
    head_count = head_width // HD
    flat_tokens = tokens.reshape(row_count, width)
    projected = jnp.dot(
        flat_tokens, w_qkv.reshape(width, 3 * head_width), preferred_element_type=jnp.float32
    )
    projected = projected.reshape(row_count, 3, head_width)
    bias_f = qv_bias.astype(jnp.float32)
    query_low = (projected[:, 0] + bias_f[0]).astype(jnp.bfloat16)
    key_low = projected[:, 1].astype(jnp.bfloat16)
    value_low = (projected[:, 2] + bias_f[1]).astype(jnp.bfloat16)
    keys_full, values_full = (
        lax.all_gather(
            key_low.reshape(seq_count, local_len, head_width), "ctx", axis=1, tiled=True
        ),
        lax.all_gather(
            value_low.reshape(seq_count, local_len, head_width), "ctx", axis=1, tiled=True
        ),
    )
    full_len = keys_full.shape[1]
    block_len = min(512, full_len)
    block_count = full_len // block_len
    query_four = query_low.reshape(seq_count, local_len, head_count, HD)
    stat_shape = (seq_count, head_count, local_len)
    four_shape = (seq_count, local_len, head_count, HD)

    def stats_step(block_idx, running):
        row_max, row_total = running
        scores = block_scores(
            query_four, split_heads(keys_full, block_idx * block_len, block_len, head_count)
        )
        new_max = jnp.maximum(row_max, jnp.max(scores, axis=-1))
        row_total = row_total * jnp.exp(row_max - new_max) + jnp.sum(
            jnp.exp(scores - new_max[..., None]), axis=-1
        )
        return (new_max, row_total)

    row_max, row_total = lax.fori_loop(
        0,
        block_count,
        stats_step,
        (jnp.full(stat_shape, -jnp.inf, jnp.float32), jnp.zeros(stat_shape, jnp.float32)),
    )

    def value_step(block_idx, attn_mixed):
        first_row = block_idx * block_len
        value_four = split_heads(values_full, first_row, block_len, head_count)
        prob_full = softmax_rows(
            block_scores(query_four, split_heads(keys_full, first_row, block_len, head_count)),
            row_max,
            row_total,
        )
        return attn_mixed + jnp.einsum(
            "shqk,skhd->sqhd",
            prob_full.astype(jnp.bfloat16),
            value_four,
            preferred_element_type=jnp.float32,
        )

    zero_four = jnp.zeros(four_shape, jnp.float32)
    attn_mixed = lax.fori_loop(0, block_count, value_step, zero_four)
    mixed_low = attn_mixed.reshape(row_count, head_width).astype(jnp.bfloat16)
    attn_part = contract_last(mixed_low, w_out)
    attn_out = lax.psum(attn_part.astype(jnp.bfloat16), "tp").astype(jnp.float32) + biases_f[:, 0]
    first_out, first_norm, first_scale = norm_forward(
        flat_tokens.astype(jnp.float32) + attn_out, gains_f[:, 0], biases_f[:, 1]
    )
    first_low = first_out.astype(jnp.bfloat16)
    inner_pre = jnp.dot(first_low, w_up, preferred_element_type=jnp.float32) + up_bias.astype(
        jnp.float32
    )
    activated, gelu_back = jax.vjp(gelu_exact, inner_pre)
    act_low = activated.astype(jnp.bfloat16)
    ffn_part = contract_last(act_low, w_down)
    ffn_out = lax.psum(ffn_part.astype(jnp.bfloat16), "tp").astype(jnp.float32) + biases_f[:, 2]
    grad_final = cotangent.reshape(row_count, width).astype(jnp.float32)
    final_out, final_norm, final_scale = norm_forward(
        first_out + ffn_out, gains_f[:, 1], biases_f[:, 3]
    )
    gain2_grad = jnp.sum(grad_final * final_norm, axis=0)
    shift2_grad = jnp.sum(grad_final, axis=0)
    grad_second = norm_backward(grad_final, final_norm, final_scale, gains_f[:, 1])
    ffn_grad_low = grad_second.astype(jnp.bfloat16)
    down_grad = contract_first(ffn_grad_low, act_low)
    down_bias_grad = jnp.sum(ffn_grad_low.astype(jnp.float32), axis=0)
    act_grad = jnp.dot(ffn_grad_low, w_down, preferred_element_type=jnp.float32)
    inner_low = gelu_back(act_grad)[0].astype(jnp.bfloat16)
    up_grad = contract_first(first_low, inner_low)
    up_bias_grad = jnp.sum(inner_low.astype(jnp.float32), axis=0)
    back_part = contract_last(inner_low, w_up)
    first_grad = grad_second + lax.psum(back_part.astype(jnp.bfloat16), "tp").astype(jnp.float32)
    gain1_grad = jnp.sum(first_grad * first_norm, axis=0)
    shift1_grad = jnp.sum(first_grad, axis=0)
    resid_grad = norm_backward(first_grad, first_norm, first_scale, gains_f[:, 0])
    attn_grad_low = resid_grad.astype(jnp.bfloat16)
    out_grad = contract_first(attn_grad_low, mixed_low)
    out_bias_grad = jnp.sum(attn_grad_low.astype(jnp.float32), axis=0)
    mixed_grad_low = jnp.dot(attn_grad_low, w_out, preferred_element_type=jnp.float32).astype(
        jnp.bfloat16
    )
    grad_four = mixed_grad_low.reshape(four_shape)
    row_delta = jnp.einsum(
        "sqhd,sqhd->shq", grad_four.astype(jnp.float32), attn_mixed, precision=highest
    )

    def grad_step(block_idx, running):
        query_grad, key_all, value_all = running
        first_row = block_idx * block_len
        key_four = split_heads(keys_full, first_row, block_len, head_count)
        value_four = split_heads(values_full, first_row, block_len, head_count)
        scores = block_scores(query_four, key_four)
        prob_low, score_low = score_grads(
            scores, row_max, row_total, row_delta, grad_four, value_four
        )
        query_grad = query_grad + jnp.einsum(
            "shqk,skhd->sqhd", score_low, key_four, preferred_element_type=jnp.float32
        )
        key_part = (
            jnp.einsum("shqk,sqhd->skhd", score_low, query_four, preferred_element_type=jnp.float32)
            * score_scale
        )
        value_part = jnp.einsum(
            "shqk,sqhd->skhd", prob_low, grad_four, preferred_element_type=jnp.float32
        )
        key_all = lax.dynamic_update_slice_in_dim(
            key_all, key_part.reshape(seq_count, block_len, head_width), first_row, 1
        )
        value_all = lax.dynamic_update_slice_in_dim(
            value_all, value_part.reshape(seq_count, block_len, head_width), first_row, 1
        )
        return (query_grad, key_all, value_all)

    zeros_full = jnp.zeros((seq_count, full_len, head_width), jnp.float32)
    query_grad, key_all, value_all = lax.fori_loop(
        0, block_count, grad_step, (zero_four, zeros_full, zeros_full)
    )
    key_grad, value_grad = (
        lax.psum_scatter(
            key_all.astype(jnp.bfloat16), "ctx", scatter_dimension=1, tiled=True
        ).astype(jnp.float32),
        lax.psum_scatter(
            value_all.astype(jnp.bfloat16), "ctx", scatter_dimension=1, tiled=True
        ).astype(jnp.float32),
    )
    query_grad_low = (query_grad * score_scale).reshape(row_count, head_width).astype(jnp.bfloat16)
    key_grad_low = key_grad.reshape(row_count, head_width).astype(jnp.bfloat16)
    value_grad_low = value_grad.reshape(row_count, head_width).astype(jnp.bfloat16)
    grad_cat = jnp.stack([query_grad_low, key_grad_low, value_grad_low], axis=1)
    qkv_grad = jnp.einsum("td,tcj->dcj", flat_tokens, grad_cat, preferred_element_type=jnp.float32)
    qv_grad = jnp.stack(
        [
            jnp.sum(query_grad_low.astype(jnp.float32), axis=0),
            jnp.sum(value_grad_low.astype(jnp.float32), axis=0),
        ]
    )
    input_part = contract_last(
        grad_cat.reshape(row_count, 3 * head_width), w_qkv.reshape(width, 3 * head_width)
    )
    gains_grad = jnp.stack([gain1_grad, gain2_grad], axis=1)
    shifts_grad = jnp.stack([shift1_grad, shift2_grad], axis=1)
    tokens_full = resid_grad + lax.psum(input_part.astype(jnp.bfloat16), "tp").astype(jnp.float32)
    tokens_share = own_rows(to_three(tokens_full))
    output_share = own_rows(to_three(final_out))
    biases_grad = jnp.stack(
        [out_bias_grad, shifts_grad[:, 0], down_bias_grad, shifts_grad[:, 1]], axis=1
    )
    shards = (
        lax.psum_scatter(qkv_grad, ("fsdp", "ctx"), scatter_dimension=0, tiled=True),
        lax.psum_scatter(out_grad, ("fsdp", "ctx"), scatter_dimension=0, tiled=True),
        lax.psum_scatter(up_grad, ("fsdp", "ctx"), scatter_dimension=0, tiled=True),
        lax.psum_scatter(down_grad, ("fsdp", "ctx"), scatter_dimension=0, tiled=True),
        lax.psum_scatter(gains_grad, ("fsdp", "ctx"), scatter_dimension=0, tiled=True),
        lax.psum_scatter(biases_grad, ("fsdp", "ctx"), scatter_dimension=0, tiled=True),
    )
    qv_total, up_total = lax.psum((qv_grad, up_bias_grad), ("fsdp", "ctx"))
    output = output_share.astype(jnp.bfloat16)
    tokens_out = tokens_share.astype(jnp.bfloat16)
    return (
        output,
        tokens_out,
        shards[0],
        qv_total,
        shards[1],
        shards[2],
        up_total,
        shards[3],
        shards[4],
        shards[5],
    )


def solution(mesh):
    in_specs = (
        P("fsdp", "ctx", None),
        P(("fsdp", "ctx"), None, "tp"),
        P(None, "tp"),
        P(("fsdp", "ctx"), "tp"),
        P(("fsdp", "ctx"), "tp"),
        P("tp"),
        P(("fsdp", "ctx"), "tp"),
        P(("fsdp", "ctx"), None),
        P(("fsdp", "ctx"), None),
        P("fsdp", "ctx", None),
    )
    out_specs = (
        P("fsdp", ("ctx", "tp"), None),
        P("fsdp", ("ctx", "tp"), None),
        P(("fsdp", "ctx"), None, "tp"),
        P(None, "tp"),
        P(("fsdp", "ctx"), "tp"),
        P(("fsdp", "ctx"), "tp"),
        P("tp"),
        P(("fsdp", "ctx"), "tp"),
        P(("fsdp", "ctx"), None),
        P(("fsdp", "ctx"), None),
    )
    return jax.shard_map(body, mesh=mesh, in_specs=in_specs, out_specs=out_specs, check_vma=False)
```

profile of v0, /device:TPU:0, one launch (start us, length us, event | category | flops | bytes accessed | tf_op | source)
XLA Modules:
  0.0 2090.9 jit_solution(9542823779875088038)
XLA Ops:
  8.0 45.5 %all-gather.8.cloned.1.call-done = bf16[768,3,384]{2,0,1:T(8,128)(2,1)} async-done(((bf16[48,3,384]{2,0,1:T(8,128)(2,1)}), bf16[768,3,384]{2,0,1:T(8,128)(2,1)}) %all-gather.8.cloned.1.call-update) | async-done | bytes 1769488 | tf_op jit(solution)/shard_map/all_gather | solution.py:94
  67.9 53.4 %all_gather.27 = bf16[768,384]{1,0:T(8,128)(2,1)} all-gather(bf16[48,384]{1,0:T(8,128)(2,1)S(1)} %copy-done.33), channel_id=1, replica_groups=mesh['fsdp'=4,'ctx'=4,'tp'=2] {'fsdp','ctx'}, dimensions={0}, use_global_device_ids=true | all-gather | bytes 626688 | tf_op jit(solution)/shard_map/all_gather | solution.py:95
  142.1 48.3 %all-gather.12.cloned.1.call-done = bf16[2,4096,384]{1,2,0:T(8,128)(2,1)} async-done(((bf16[2,1024,384]{1,2,0:T(8,128)(2,1)}), bf16[2,4096,384]{1,2,0:T(8,128)(2,1)}) %all-gather.12.cloned.1.call-update) | async-done | bytes 6291472 | tf_op jit(solution)/shard_map/all_gather | solution.py:116
  190.4 93.1 %while.48 = (s32[]{:T(128)}, f32[2,6,1024]{2,1,0:T(8,128)S(1)}, f32[2,6,1024]{2,1,0:T(8,128)S(1)}, bf16[2,4096,384]{1,2,0:T(8,128)(2,1)}, bf16[2,1024,6,64]{1,3,...) while((s32[]{:T(128)}, f32[2,6,1024]{2,1,0:T(8,128)S(1)}, ...), condition=%wide.region_3.0_spmd.clone, body=%wide.region_0.0_spmd.clone.sunk | while | flops 836825088 | bytes 54902944 | solution.py:141
  283.4 22.7 %all-gather.10.cloned.1.call-done = bf16[2,4096,384]{1,2,0:T(8,128)(2,1)} async-done(((bf16[2,1024,384]{1,2,0:T(8,128)(2,1)}), bf16[2,4096,384]{1,2,0:T(8,128)(2,1)}) %all-gather.10.cloned.1.call-update) | async-done | bytes 6291472 | tf_op jit(solution)/shard_map/all_gather | solution.py:119
  306.2 88.7 %while.49 = (s32[]{:T(128)}, f32[2,1024,6,64]{1,3,2,0:T(8,128)}, bf16[2,4096,384]{1,2,0:T(8,128)(2,1)}, bf16[2,4096,384]{1,2,0:T(8,128)(2,1)}, bf16[2,1024,6,64]...) while((s32[]{:T(128)}, f32[2,1024,6,64]{1,3,2,0:T(8,128)}, ...), condition=%wide.region_5.0_spmd.clone, body=%wide.region_4.0_spmd.clone.sunk | while | flops 1637351424 | bytes 12681393 | solution.py:164
  405.1 29.4 %all-gather.1 = bf16[16,48,2]{1,2,0:T(2,128)(2,1)S(1)} all-gather(bf16[1,48,2]{1,2,0:T(2,128)(2,1)S(1)} %bitcast.191), channel_id=1, replica_groups=mesh['fsdp'=4,'ctx'=4,'tp'=2] {'fsdp','ctx'}, dimensions={0}, use_global_device_ids=true | all-gather | bytes 3264 | tf_op jit(solution)/shard_map/all_gather | solution.py:98
  434.7 29.8 %all-gather = bf16[16,48,4]{1,2,0:T(4,128)(2,1)S(1)} all-gather(bf16[1,48,4]{1,2,0:T(4,128)(2,1)S(1)} %bitcast.190), channel_id=1, replica_groups=mesh['fsdp'=4,'ctx'=4,'tp'=2] {'fsdp','ctx'}, dimensions={0}, use_global_device_ids=true | all-gather | bytes 6528 | tf_op jit(solution)/shard_map/all_gather | solution.py:99
  465.2 22.8 %all-reduce.8.cloned.1.call-done = bf16[2048,768]{1,0:T(8,128)(2,1)} async-done(((bf16[2048,768]{1,0:T(8,128)(2,1)}), bf16[2048,768]{1,0:T(8,128)(2,1)}) %all-reduce.8.cloned.1.call-update) | async-done | bytes 3145744 | tf_op jit(solution)/shard_map/psum | solution.py:167
  496.9 35.6 %all-gather.14.cloned.1.call-done = bf16[768,1536]{1,0:T(8,128)(2,1)} async-done(((bf16[48,1536]{1,0:T(8,128)(2,1)}), bf16[768,1536]{1,0:T(8,128)(2,1)}) %all-gather.14.cloned.1.call-update) | async-done | bytes 2359312 | tf_op jit(solution)/shard_map/all_gather | solution.py:96
  532.5 35.1 %multiply_convert_fusion.1 = (bf16[2048,1536]{1,0:T(8,128)(2,1)}, f32[2048,1536]{1,0:T(8,128)}, f32[2048,1536]{1,0:T(8,128)}) fusion(f32[1536]{0:T(1024)S(1)} %convert_element_type.186, bf16[768,1536]{1,0:T(8,128)(2,1)} %all-gather.14.cloned.1.call-done, f32[2048,768]{1,0:T(8,128)} %subtract_multiply_fusion.2, f32[768]{0:T(1024)S(1)} %get-tuple-element.637, ...), kind=kOutput, calls=%fused_computation.29 | convolution fusion | flops 5044174848 | bytes 40120320 | tf_op jit(solution)/shard_map/dot_general | solution.py:172
  587.0 82.7 %all-reduce.10.cloned.1.call-done = bf16[2048,768]{1,0:T(8,128)(2,1)} async-done(((bf16[2048,768]{1,0:T(8,128)(2,1)}), bf16[2048,768]{1,0:T(8,128)(2,1)}) %all-reduce.10.cloned.1.call-update) | async-done | bytes 3145744 | tf_op jit(solution)/shard_map/psum | solution.py:178
  681.4 18.9 convert_reduce_fusion
  709.4 85.9 %all-reduce.12.cloned.1.call-done = bf16[2048,768]{1,0:T(8,128)(2,1)} async-done(((bf16[2048,768]{1,0:T(8,128)(2,1)}), bf16[2048,768]{1,0:T(8,128)(2,1)}) %all-reduce.12.cloned.1.call-update) | async-done | bytes 3145744 | tf_op jit(solution)/shard_map/psum | solution.py:194
  830.2 482.1 %while.50 = (s32[]{:T(128)}, f32[2,1024,6,64]{1,3,2,0:T(8,128)}, bf16[2,4096,384]{1,2,0:T(8,128)(2,1)}, bf16[2,4096,384]{1,2,0:T(8,128)(2,1)}, bf16[2,4096,384]{...) while((s32[]{:T(128)}, f32[2,1024,6,64]{1,3,2,0:T(8,128)}, ...), condition=%wide.region_18.0_spmd.clone, body=%wide.region_17.0_spmd.clone.sunk | while | flops 4072931328 | bytes 139346160 | solution.py:237
  856.5 14.5 multiply_convert_fusion.5
  915.8 14.5 multiply_convert_fusion.5
  976.1 14.5 multiply_convert_fusion.5
  1036.4 14.5 multiply_convert_fusion.5
  1096.7 14.5 multiply_convert_fusion.5
  1157.1 14.5 multiply_convert_fusion.5
  1217.5 14.5 multiply_convert_fusion.5
  1277.9 14.5 multiply_convert_fusion.5
  1328.0 95.3 %reduce-scatter.12.cloned.1.call-done = bf16[2,1024,384]{1,2,0:T(8,128)(2,1)} async-done(((bf16[2,4096,384]{1,2,0:T(8,128)(2,1)}), bf16[2,1024,384]{1,2,0:T(8,128)(2,1)}) %reduce-scatter.12.cloned.1.call-update) | async-done | bytes 1572880 | tf_op jit(solution)/shard_map/reduce_scatter | solution.py:241
  1425.9 110.9 %reduce-scatter.14.cloned.1.call-done = bf16[2,1024,384]{1,2,0:T(8,128)(2,1)} async-done(((bf16[2,4096,384]{1,2,0:T(8,128)(2,1)}), bf16[2,1024,384]{1,2,0:T(8,128)(2,1)}) %reduce-scatter.14.cloned.1.call-update) | async-done | bytes 1572880 | tf_op jit(solution)/shard_map/reduce_scatter | solution.py:244
  1598.2 57.1 %reduce-scatter.24.cloned.1.call-done = f32[48,4]{1,0:T(8,128)} async-done(((f32[768,4]{1,0:T(8,128)}), f32[48,4]{1,0:T(8,128)}) %reduce-scatter.24.cloned.1.call-update) | async-done | bytes 784
  1656.9 61.1 %all-reduce.1 = (f32[2,384]{1,0:T(2,128)}, f32[1536]{0:T(1024)}) all-reduce(f32[2,384]{1,0:T(2,128)S(1)} %pad_maximum_fusion.5, f32[1536]{0:T(1024)S(1)} %copy-done.43), channel_id=1, replica_groups=mesh['fsdp'=4,'ctx'=4,'tp'=2] {'fsdp','ctx'}, use_global_device_ids=true, to_apply=%region_25.0 | all-reduce | flops 2304 | bytes 18432 | tf_op jit(solution)/shard_map/psum | solution.py:278
  1718.1 58.1 %all-reduce.16.cloned.1.call-done = f32[768,3,384]{2,1,0:T(4,128)} async-done(((f32[768,3,384]{2,1,0:T(4,128)}), f32[768,3,384]{2,1,0:T(4,128)}) %all-reduce.16.cloned.1.call-update) | async-done | bytes 3538960
  1777.8 86.1 %all-reduce.14.cloned.1.call-done = bf16[2048,768]{1,0:T(8,128)(2,1)} async-done(((bf16[2048,768]{1,0:T(8,128)(2,1)}), bf16[2048,768]{1,0:T(8,128)(2,1)}) %all-reduce.14.cloned.1.call-update) | async-done | bytes 3145744 | tf_op jit(solution)/shard_map/psum | solution.py:264
  1869.6 56.6 %reduce-scatter.16.cloned.1.call-done = f32[48,384]{1,0:T(8,128)} async-done(((f32[768,384]{1,0:T(8,128)}), f32[48,384]{1,0:T(8,128)}) %reduce-scatter.16.cloned.1.call-update) | async-done | bytes 73744 | tf_op jit(solution)/shard_map/reduce_scatter | solution.py:272
  1926.2 78.9 %reduce-scatter.20.cloned.1.call-done = f32[48,1536]{1,0:T(8,128)} async-done(((f32[768,1536]{1,0:T(8,128)}), f32[48,1536]{1,0:T(8,128)}) %reduce-scatter.20.cloned.1.call-update) | async-done | bytes 294928 | tf_op jit(solution)/shard_map/reduce_scatter | solution.py:274
  2005.0 79.2 %reduce-scatter.18.cloned.1.call-done = f32[48,1536]{1,0:T(8,128)} async-done(((f32[768,1536]{1,0:T(8,128)}), f32[48,1536]{1,0:T(8,128)}) %reduce-scatter.18.cloned.1.call-update) | async-done | bytes 294928 | tf_op jit(solution)/shard_map/reduce_scatter | solution.py:273
  (360 shorter events, 764.9 us)
Async XLA Ops:
  7.2 46.2 %all-gather.8.cloned.1.call-start = ((), (), s32[]{:S(2)}) async-start(), calls=%async_computation.7 | async-start | bytes 1880064 | tf_op jit(solution)/shard_map/all_gather | solution.py:94
  7.9 182.5 %all-gather.12.cloned.1.call-start = ((), (), s32[]{:S(2)}) async-start(), calls=%async_computation.9 | async-start | bytes 7864320 | tf_op jit(solution)/shard_map/all_gather | solution.py:116
  67.7 238.5 %all-gather.10.cloned.1.call-start = ((), (), s32[]{:S(2)}) async-start(), calls=%async_computation.8 | async-start | bytes 7864320 | tf_op jit(solution)/shard_map/all_gather | solution.py:119
  141.9 346.1 %all-reduce.8.cloned.1.call-start = ((), (), s32[]{:S(2)}) async-start(), calls=%async_computation.10 | async-start | bytes 6291456 | tf_op jit(solution)/shard_map/psum | solution.py:167
  400.4 34.3 %copy-start.46 = (bf16[48,4]{0,1:T(4,128)(2,1)S(1)}, bf16[48,4]{0,1:T(4,128)(2,1)}, u32[]{:S(2)}) copy-start(bf16[48,4]{0,1:T(4,128)(2,1)} %param.24) | copy-start | bytes 1156
  400.4 87.7 %copy-start.7 = (bf16[2,1024,768]{2,1,0:T(8,128)(2,1)S(1)}, bf16[2,1024,768]{2,1,0:T(8,128)(2,1)}, u32[]{:S(2)}) copy-start(bf16[2,1024,768]{2,1,0:T(8,128)(2,1)} %param.16) | copy-start | bytes 9437188
  403.9 128.7 %all-gather.14.cloned.1.call-start = ((), (), s32[]{:S(2)}) async-start(), calls=%async_computation.11 | async-start | bytes 2506752 | tf_op jit(solution)/shard_map/all_gather | solution.py:96
  404.4 171.3 %all-gather.16.cloned.1.call-start = ((), (), s32[]{:S(2)}) async-start(), calls=%async_computation.12 | async-start | bytes 2506752 | tf_op jit(solution)/shard_map/all_gather | solution.py:97
  405.0 264.7 %all-reduce.10.cloned.1.call-start = ((), (), s32[]{:S(2)}) async-start(), calls=%async_computation.13 | async-start | bytes 6291456 | tf_op jit(solution)/shard_map/psum | solution.py:178
  434.6 244.5 %copy-start.27 = (f32[768]{0:T(1024)}, f32[768]{0:T(1024)S(1)}, u32[]{:S(2)}) copy-start(f32[768]{0:T(1024)S(1)} %get-tuple-element.639) | copy-start | bytes 9220
  434.7 370.4 %copy-start.31 = (f32[768]{0:T(1024)}, f32[768]{0:T(1024)S(1)}, u32[]{:S(2)}) copy-start(f32[768]{0:T(1024)S(1)} %get-tuple-element.640) | copy-start | bytes 9220
  465.2 204.5 %copy-start.35 = (f32[768]{0:T(1024)}, f32[768]{0:T(1024)S(1)}, u32[]{:S(2)}) copy-start(f32[768]{0:T(1024)S(1)} %get-tuple-element.637) | copy-start | bytes 9220
  585.0 210.3 %all-reduce.12.cloned.1.call-start = ((), (), s32[]{:S(2)}) async-start(), calls=%async_computation.14 | async-start | bytes 6291456 | tf_op jit(solution)/shard_map/psum | solution.py:194
  681.4 18.9 copy-start.4
  709.3 713.9 %reduce-scatter.12.cloned.1.call-start = ((), (), s32[]{:S(2)}) async-start(), calls=%async_computation.15 | async-start | bytes 7864320 | tf_op jit(solution)/shard_map/reduce_scatter | solution.py:241
  709.4 95.6 %copy-start.30 = (f32[2048]{0:T(1024)S(1)}, f32[2048]{0:T(1024)}, u32[]{:S(2)}) copy-start(f32[2048]{0:T(1024)} %copy-done.29) | copy-start | bytes 24580
  1312.3 224.4 %reduce-scatter.14.cloned.1.call-start = ((), (), s32[]{:S(2)}) async-start(), calls=%async_computation.16 | async-start | bytes 7864320 | tf_op jit(solution)/shard_map/reduce_scatter | solution.py:244
  1312.9 283.8 %reduce-scatter.22.cloned.1.call-start = ((), (), s32[]{:S(2)}) async-start(), calls=%async_computation.21 | async-start | bytes 417792
  1315.6 339.6 %reduce-scatter.24.cloned.1.call-start = ((), (), s32[]{:S(2)}) async-start(), calls=%async_computation.22 | async-start | bytes 417792
  1321.4 217.9 %copy-start.8 = (bf16[2,1024,768]{2,1,0:T(8,128)(2,1)S(1)}, bf16[2,1024,768]{2,1,0:T(8,128)(2,1)}, u32[]{:S(2)}) copy-start(bf16[2,1024,768]{2,1,0:T(8,128)(2,1)} %param.16) | copy-start | bytes 9437188
  1327.9 448.2 %all-reduce.16.cloned.1.call-start = ((), (), s32[]{:S(2)}) async-start(), calls=%async_computation.23 | async-start | bytes 9437184
  1553.8 310.0 %all-reduce.14.cloned.1.call-start = ((), (), s32[]{:S(2)}) async-start(), calls=%async_computation.17 | async-start | bytes 6291456 | tf_op jit(solution)/shard_map/psum | solution.py:264
  1562.5 363.6 %reduce-scatter.16.cloned.1.call-start = ((), (), s32[]{:S(2)}) async-start(), calls=%async_computation.18 | async-start | bytes 1253376 | tf_op jit(solution)/shard_map/reduce_scatter | solution.py:272
  1568.4 436.6 %reduce-scatter.20.cloned.1.call-start = ((), (), s32[]{:S(2)}) async-start(), calls=%async_computation.20 | async-start | bytes 5013504 | tf_op jit(solution)/shard_map/reduce_scatter | solution.py:274
  1579.0 10.7 copy-start.48
  1579.0 11.9 copy-start.24
  1579.0 11.9 copy-start.26
  1579.0 11.9 copy-start.28
  1579.0 11.9 copy-start.34
  1579.0 505.2 %reduce-scatter.18.cloned.1.call-start = ((), (), s32[]{:S(2)}) async-start(), calls=%async_computation.19 | async-start | bytes 5013504 | tf_op jit(solution)/shard_map/reduce_scatter | solution.py:273
  1590.9 65.7 %copy-start.15 = (bf16[2,1024,384]{1,2,0:T(8,128)(2,1)S(1)}, bf16[2,1024,384]{1,2,0:T(8,128)(2,1)}, u32[]{:S(2)}) copy-start(bf16[2,1024,384]{1,2,0:T(8,128)(2,1)} %reduce-scatter.14.cloned.1.call-done) | copy-start | bytes 4718596
  1590.9 66.0 %copy-start.43 = (f32[1536]{0:T(1024)S(1)}, f32[1536]{0:T(1024)}, u32[]{:S(2)}) copy-start(f32[1536]{0:T(1024)} %get-tuple-element.708) | copy-start | bytes 18436
  (41 other events, 230.5 us)
Sparse Core Ops, SparseCore 0:
  10.2 43.1 all-gather.7
  67.8 122.5 all-gather.11
  192.5 113.6 all-gather.9
  404.0 83.9 all-reduce.7
  490.2 42.3 all-gather.13
  534.7 41.0 all-gather.15
  585.1 84.5 all-reduce.9
  709.5 85.8 all-reduce.11
  1312.5 110.7 reduce-scatter.11
  1425.4 111.2 reduce-scatter.13
  1540.2 56.4 reduce-scatter.21
  1600.1 55.0 reduce-scatter.23
  1658.8 117.2 all-reduce.15
  1778.3 85.5 all-reduce.13
  1867.9 58.1 reduce-scatter.15
  1930.4 74.5 reduce-scatter.19
  2009.3 74.8 reduce-scatter.17
where the time goes:
time: 2100 us; the launch traced here: 2090 us
  waiting for transfers between devices  977 us (47%)
  matrix products  697 us (33%)
  blocking collectives  174 us (8%)
  local copies, waits for them, and re-layouts  134 us (6%)
  other arithmetic  92 us (4%)
    dot_general x16, matrix products, block_scores(): jnp.einsum('sqhd,skhd->shqk', query_four, key_four, preferred_element_typ...  141 us
    unnamed x20, waiting for transfers between devices  119 us
    dot_general x8, matrix products, score_grads(): jnp.einsum('sqhd,skhd->shqk', grad_four, value_four, preferred_element_ty...  116 us
    reduce_scatter x1, waiting for transfers between devices, body(): lax.psum_scatter(value_all.astype(jnp.bfloat16), 'ctx', scatter_dimension...  111 us
    reduce_scatter x1, waiting for transfers between devices, body(): lax.psum_scatter(key_all.astype(jnp.bfloat16), 'ctx', scatter_dimension=1...  95.3 us
    dot_general x8, matrix products, grad_step(): jnp.einsum('shqk,sqhd->skhd', prob_low, grad_four, preferred_element_type...  89.2 us
    psum x1, waiting for transfers between devices, body(): lax.psum(input_part.astype(jnp.bfloat16), 'tp').astype(jnp.float32)  86.1 us
    psum x1, waiting for transfers between devices, body(): lax.psum(back_part.astype(jnp.bfloat16), 'tp').astype(jnp.float32)  85.9 us
  transfers between devices with their start and end apart: 17, of which 17 were waited for; matrix products, arithmetic and copies ran while one was open for 12% of the time, Pallas kernels for 0%

commit v1 on v0

--- a/solution.py
+++ b/solution.py
@@ -7,6 +7,18 @@
 epsilon = 1e-12
 score_scale = 0.125
 highest = lax.Precision.HIGHEST
+
+
+def collect(x, axis, dim):
+    ways, here = (lax.axis_size(axis), lax.axis_index(axis))
+    grown, reach = (x, 1)
+    while reach < ways:
+        theirs = lax.ppermute(grown, axis, [(d, d ^ reach) for d in range(ways)])
+        mine_first = jnp.concatenate([grown, theirs], axis=dim)
+        theirs_first = jnp.concatenate([theirs, grown], axis=dim)
+        grown = jnp.where(here & reach == 0, mine_first, theirs_first)
+        reach = 2 * reach
+    return grown
 
 
 def contract_last(left, right):
@@ -91,7 +103,7 @@
         return array_two.reshape(seq_count, array_two.shape[0] // seq_count, array_two.shape[1])
 
     gathered = (
-        lax.all_gather(qkv_weight, ("fsdp", "ctx"), axis=0, tiled=True),
+        collect(qkv_weight, ("fsdp", "ctx"), 0),
         lax.all_gather(out_weight, ("fsdp", "ctx"), axis=0, tiled=True),
         lax.all_gather(up_weight, ("fsdp", "ctx"), axis=0, tiled=True),
         lax.all_gather(down_weight, ("fsdp", "ctx"), axis=0, tiled=True),

time: 2100 us -> 1950 us (0.929)
  waiting for transfers between devices: 977 us -> 704 us
  other arithmetic: 92 us -> 154 us
  matrix products: 697 us -> 727 us
    reduce_scatter x1, waiting for transfers between devices: 56.6 us -> 0.01 us  [body(): lax.psum_scatter(out_grad, ('fsdp', 'ctx'), scatter_dimension=0, tiled=True)]
    psum x1, waiting for transfers between devices: 86.1 us -> 31.7 us  [body(): lax.psum(input_part.astype(jnp.bfloat16), 'tp').astype(jnp.float32)]
    reduce_sum x8, other arithmetic: 34.4 us -> 83.8 us  [stats_step(): jnp.sum(jnp.exp(scores - new_max[..., None]), axis=-1)]
    unnamed x20 -> x19, waiting for transfers between devices: 119 us -> 69.5 us
    all_gather x1 -> x0, waiting for transfers between devices: 45.5 us -> none  [body(): lax.all_gather(qkv_weight, ('fsdp', 'ctx'), axis=0, tiled=True)]
    dot_general x16, matrix products: 141 us -> 181 us  [block_scores(): jnp.einsum('sqhd,skhd->shqk', query_four, key_four, preferred_element_typ...]
    reduce_scatter x1, waiting for transfers between devices: 78.9 us -> 40.1 us  [body(): lax.psum_scatter(down_grad, ('fsdp', 'ctx'), scatter_dimension=0, tiled=T...]
    ppermute x0 -> x4, waiting for transfers between devices: none -> 35.7 us  [collect(): theirs = lax.ppermute(grown, axis, [(d, d ^ reach) for d in range(ways)])]
  transfers between devices with their start and end apart: 17 -> 20, of which waited for: 17 -> 15; matrix products, arithmetic and copies ran while one was open for 12% -> 18% of each run, Pallas kernels for 0% -> 0%
where the time goes in v1:
time: 1950 us; the launch traced here: 1940 us
  matrix products  727 us (37%)
  waiting for transfers between devices  704 us (36%)
  blocking collectives  176 us (9%)
  other arithmetic  154 us (8%)
  local copies, waits for them, and re-layouts  150 us (8%)
    dot_general x16, matrix products, block_scores(): jnp.einsum('sqhd,skhd->shqk', query_four, key_four, preferred_element_typ...  181 us
    dot_general x8, matrix products, score_grads(): jnp.einsum('sqhd,skhd->shqk', grad_four, value_four, preferred_element_ty...  116 us
    reduce_scatter x1, waiting for transfers between devices, body(): lax.psum_scatter(value_all.astype(jnp.bfloat16), 'ctx', scatter_dimension...  111 us
    reduce_scatter x1, waiting for transfers between devices, body(): lax.psum_scatter(key_all.astype(jnp.bfloat16), 'ctx', scatter_dimension=1...  95.2 us
    psum x1, waiting for transfers between devices, body(): lax.psum(back_part.astype(jnp.bfloat16), 'tp').astype(jnp.float32)  85.7 us
    reduce_sum x8, other arithmetic, stats_step(): jnp.sum(jnp.exp(scores - new_max[..., None]), axis=-1)  83.8 us
    psum x1, waiting for transfers between devices, body(): lax.psum(ffn_part.astype(jnp.bfloat16), 'tp').astype(jnp.float32)  83.5 us
    dot_general x8, matrix products, grad_step(): jnp.einsum('shqk,sqhd->skhd', prob_low, grad_four, preferred_element_type...  82.4 us
  transfers between devices with their start and end apart: 20, of which 15 were waited for; matrix products, arithmetic and copies ran while one was open for 18% of the time, Pallas kernels for 0%

profile of v1, /device:TPU:0, one launch (start us, length us, event | category | flops | bytes accessed | tf_op | source)
XLA Modules:
  0.0 1939.0 jit_solution(15432669599757194950)
XLA Ops:
  23.1 13.0 collective-permute-done.1
  56.8 13.6 collective-permute-done.3
  84.2 55.4 %all_gather.23 = bf16[768,384]{1,0:T(8,128)(2,1)} all-gather(bf16[48,384]{1,0:T(8,128)(2,1)S(1)} %copy-done.35), channel_id=1, replica_groups=mesh['fsdp'=4,'ctx'=4,'tp'=2] {'fsdp','ctx'}, dimensions={0}, use_global_device_ids=true | all-gather | bytes 626688 | tf_op jit(solution)/shard_map/all_gather | solution.py:107
  158.9 49.4 %all-gather.9.cloned.1.call-done = bf16[2,4096,384]{2,1,0:T(8,128)(2,1)} async-done(((bf16[2,1024,384]{2,1,0:T(8,128)(2,1)}), bf16[2,4096,384]{2,1,0:T(8,128)(2,1)}) %all-gather.9.cloned.1.call-update) | async-done | bytes 6291472 | tf_op jit(solution)/shard_map/all_gather | solution.py:128
  217.2 175.3 %while.48 = (s32[]{:T(128)}, f32[2,6,1024]{2,1,0:T(8,128)S(1)}, f32[2,6,1024]{2,1,0:T(8,128)S(1)}, bf16[2,4096,384]{1,2,0:T(8,128)(2,1)}, bf16[2,1024,6,64]{1,3,...) while((s32[]{:T(128)}, f32[2,6,1024]{2,1,0:T(8,128)S(1)}, ...), condition=%wide.region_3.4_spmd.clone, body=%wide.region_0.3_spmd.clone.sunk | while | flops 836825088 | bytes 54902936 | solution.py:153
  401.3 85.8 %while.49 = (s32[]{:T(128)}, f32[2,1024,6,64]{1,3,2,0:T(8,128)}, bf16[2,4096,384]{1,2,0:T(8,128)(2,1)}, bf16[2,4096,384]{1,2,0:T(8,128)(2,1)}, bf16[2,1024,6,64]...) while((s32[]{:T(128)}, f32[2,1024,6,64]{1,3,2,0:T(8,128)}, ...), condition=%wide.region_5.6_spmd.clone, body=%wide.region_4.5_spmd.clone.sunk | while | flops 1637351424 | bytes 12681385 | solution.py:176
  497.9 30.4 %all-gather = bf16[16,48,4]{1,2,0:T(4,128)(2,1)S(1)} all-gather(bf16[1,48,4]{1,2,0:T(4,128)(2,1)S(1)} %bitcast.198), channel_id=1, replica_groups=mesh['fsdp'=4,'ctx'=4,'tp'=2] {'fsdp','ctx'}, dimensions={0}, use_global_device_ids=true | all-gather | bytes 6528 | tf_op jit(solution)/shard_map/all_gather | solution.py:111
  529.0 29.2 %all-gather.1 = bf16[16,48,2]{1,2,0:T(2,128)(2,1)S(1)} all-gather(bf16[1,48,2]{1,2,0:T(2,128)(2,1)S(1)} %bitcast.199), channel_id=1, replica_groups=mesh['fsdp'=4,'ctx'=4,'tp'=2] {'fsdp','ctx'}, dimensions={0}, use_global_device_ids=true | all-gather | bytes 3264 | tf_op jit(solution)/shard_map/all_gather | solution.py:110
  558.4 23.3 %all-reduce.8.cloned.1.call-done = bf16[2048,768]{1,0:T(8,128)(2,1)} async-done(((bf16[2048,768]{1,0:T(8,128)(2,1)}), bf16[2048,768]{1,0:T(8,128)(2,1)}) %all-reduce.8.cloned.1.call-update) | async-done | bytes 3145744 | tf_op jit(solution)/shard_map/psum | solution.py:179
  591.9 35.1 %multiply_convert_fusion.1 = (bf16[2048,1536]{1,0:T(8,128)(2,1)}, f32[2048,1536]{1,0:T(8,128)}, f32[2048,1536]{1,0:T(8,128)}) fusion(f32[1536]{0:T(1024)S(1)} %convert_element_type.186, bf16[768,1536]{1,0:T(8,128)(2,1)} %all-gather.11.cloned.1.call-done, f32[2048,768]{1,0:T(8,128)} %subtract_multiply_fusion.2, f32[768]{0:T(1024)S(1)} %get-tuple-element.637, ...), kind=kOutput, calls=%fused_computation.29 | convolution fusion | flops 5044174848 | bytes 40120320 | tf_op jit(solution)/shard_map/dot_general | solution.py:184
  638.7 83.5 %all-reduce.10.cloned.1.call-done = bf16[2048,768]{1,0:T(8,128)(2,1)} async-done(((bf16[2048,768]{1,0:T(8,128)(2,1)}), bf16[2048,768]{1,0:T(8,128)(2,1)}) %all-reduce.10.cloned.1.call-update) | async-done | bytes 3145744 | tf_op jit(solution)/shard_map/psum | solution.py:190
  733.6 18.8 convert_reduce_fusion
  761.8 85.7 %all-reduce.12.cloned.1.call-done = bf16[2048,768]{1,0:T(8,128)(2,1)} async-done(((bf16[2048,768]{1,0:T(8,128)(2,1)}), bf16[2048,768]{1,0:T(8,128)(2,1)}) %all-reduce.12.cloned.1.call-update) | async-done | bytes 3145744 | tf_op jit(solution)/shard_map/psum | solution.py:206
  882.1 474.3 %while.50 = (s32[]{:T(128)}, f32[2,1024,6,64]{1,3,2,0:T(8,128)}, bf16[2,4096,384]{1,2,0:T(8,128)(2,1)}, bf16[2,4096,384]{1,2,0:T(8,128)(2,1)}, bf16[2,4096,384]{...) while((s32[]{:T(128)}, f32[2,1024,6,64]{1,3,2,0:T(8,128)}, ...), condition=%wide.region_18.19_spmd.clone, body=%wide.region_17.18_spmd.clone.sunk | while | flops 4072931328 | bytes 136200400 | solution.py:249
  883.5 12.5 exponential_divide_fusion.2
  897.2 14.5 multiply_convert_fusion.5
  955.6 14.5 multiply_convert_fusion.5
  1001.3 12.5 exponential_divide_fusion.2
  1015.0 14.5 multiply_convert_fusion.5
  1060.7 12.5 exponential_divide_fusion.2
  1074.4 14.5 multiply_convert_fusion.5
  1133.9 14.5 multiply_convert_fusion.5
  1193.3 14.5 multiply_convert_fusion.5
  1252.7 14.5 multiply_convert_fusion.5
  1312.0 14.5 multiply_convert_fusion.5
  1372.3 95.2 %reduce-scatter.12.cloned.1.call-done = bf16[2,1024,384]{1,2,0:T(8,128)(2,1)} async-done(((bf16[2,4096,384]{1,2,0:T(8,128)(2,1)}), bf16[2,1024,384]{1,2,0:T(8,128)(2,1)}) %reduce-scatter.12.cloned.1.call-update) | async-done | bytes 1572880 | tf_op jit(solution)/shard_map/reduce_scatter | solution.py:253
  1470.1 111.0 %reduce-scatter.14.cloned.1.call-done = bf16[2,1024,384]{1,2,0:T(8,128)(2,1)} async-done(((bf16[2,4096,384]{1,2,0:T(8,128)(2,1)}), bf16[2,1024,384]{1,2,0:T(8,128)(2,1)}) %reduce-scatter.14.cloned.1.call-update) | async-done | bytes 1572880 | tf_op jit(solution)/shard_map/reduce_scatter | solution.py:256
  1647.5 62.6 %reduce-scatter.24.cloned.1.call-done = f32[48,4]{1,0:T(8,128)} async-done(((f32[768,4]{1,0:T(8,128)}), f32[48,4]{1,0:T(8,128)}) %reduce-scatter.24.cloned.1.call-update) | async-done | bytes 784
  1711.8 61.1 %all-reduce.1 = (f32[2,384]{1,0:T(2,128)}, f32[1536]{0:T(1024)}) all-reduce(f32[2,384]{1,0:T(2,128)S(1)} %pad_maximum_fusion.5, f32[1536]{0:T(1024)S(1)} %copy-done.45), channel_id=1, replica_groups=mesh['fsdp'=4,'ctx'=4,'tp'=2] {'fsdp','ctx'}, use_global_device_ids=true, to_apply=%region_25.26 | all-reduce | flops 2304 | bytes 18432 | tf_op jit(solution)/shard_map/psum | solution.py:290
  1774.6 31.7 %all-reduce.14.cloned.1.call-done = bf16[2048,768]{1,0:T(8,128)(2,1)} async-done(((bf16[2048,768]{1,0:T(8,128)(2,1)}), bf16[2048,768]{1,0:T(8,128)(2,1)}) %all-reduce.14.cloned.1.call-update) | async-done | bytes 3145744 | tf_op jit(solution)/shard_map/psum | solution.py:276
  1812.0 40.1 %reduce-scatter.20.cloned.1.call-done = f32[48,1536]{1,0:T(8,128)} async-done(((f32[768,1536]{1,0:T(8,128)}), f32[48,1536]{1,0:T(8,128)}) %reduce-scatter.20.cloned.1.call-update) | async-done | bytes 294928 | tf_op jit(solution)/shard_map/reduce_scatter | solution.py:286
  1852.1 79.1 %reduce-scatter.18.cloned.1.call-done = f32[48,1536]{1,0:T(8,128)} async-done(((f32[768,1536]{1,0:T(8,128)}), f32[48,1536]{1,0:T(8,128)}) %reduce-scatter.18.cloned.1.call-update) | async-done | bytes 294928 | tf_op jit(solution)/shard_map/reduce_scatter | solution.py:285
  (369 shorter events, 848.6 us)
Async XLA Ops:
  8.0 41.8 %copy-start.24 = (bf16[48,3,384]{2,0,1:T(8,128)(2,1)S(1)}, bf16[48,3,384]{2,0,1:T(8,128)(2,1)}, u32[]{:S(2)}) copy-start(bf16[48,3,384]{2,0,1:T(8,128)(2,1)} %param.17) | copy-start | bytes 331780
  8.0 200.3 %all-gather.9.cloned.1.call-start = ((), (), s32[]{:S(2)}) async-start(), calls=%async_computation.8 | async-start | bytes 7864320 | tf_op jit(solution)/shard_map/all_gather | solution.py:128
  9.2 10.1 collective-permute-start
  20.4 52.2 %copy-start.7 = (bf16[2,1024,768]{2,1,0:T(8,128)(2,1)S(1)}, bf16[2,1024,768]{2,1,0:T(8,128)(2,1)}, u32[]{:S(2)}) copy-start(bf16[2,1024,768]{2,1,0:T(8,128)(2,1)} %param.16) | copy-start | bytes 9437188
  20.4 15.7 collective-permute-start.1
  40.8 2.1 collective-permute-start.2
  48.4 22.0 %collective-permute-start.3 = (bf16[384,3,384]{0,2,1:T(8,128)(2,1)}, bf16[384,3,384]{0,2,1:T(8,128)(2,1)}, u32[]{:S(2)}, u32[]{:S(2)}) collective-permute-start(bf16[384,3,384]{0,2,1:T(8,128)(2,1)} %maximum_select_fusion.5), channel_id=1, source_target_pairs={{0,16},{2,18},{4,20},{6,22},{8,24},{10,26},{12,28},{14,30},{16,0},... | collective-permute-start | bytes 2654216 | tf_op jit(solution)/shard_map/ppermute | solution.py:16
  84.0 308.5 %all-gather.7.cloned.1.call-start = ((), (), s32[]{:S(2)}) async-start(), calls=%async_computation.7 | async-start | bytes 7864320 | tf_op jit(solution)/shard_map/all_gather | solution.py:131
  158.9 422.8 %all-reduce.8.cloned.1.call-start = ((), (), s32[]{:S(2)}) async-start(), calls=%async_computation.9 | async-start | bytes 6291456 | tf_op jit(solution)/shard_map/psum | solution.py:179
  493.1 35.9 %copy-start.49 = (bf16[48,2]{0,1:T(2,128)(2,1)S(1)}, bf16[48,2]{0,1:T(2,128)(2,1)}, u32[]{:S(2)}) copy-start(bf16[48,2]{0,1:T(2,128)(2,1)} %param.23) | copy-start | bytes 580
  493.1 65.3 %copy-start.46 = (bf16[1536]{0:T(1024)(128)(2,1)S(1)}, bf16[1536]{0:T(1024)(128)(2,1)}, u32[]{:S(2)}) copy-start(bf16[1536]{0:T(1024)(128)(2,1)} %param.21) | copy-start | bytes 9220
  496.6 89.2 %copy-start.8 = (bf16[2,1024,768]{2,1,0:T(8,128)(2,1)S(1)}, bf16[2,1024,768]{2,1,0:T(8,128)(2,1)}, u32[]{:S(2)}) copy-start(bf16[2,1024,768]{2,1,0:T(8,128)(2,1)} %param.16) | copy-start | bytes 9437188
  496.7 95.3 %all-gather.11.cloned.1.call-start = ((), (), s32[]{:S(2)}) async-start(), calls=%async_computation.10 | async-start | bytes 2506752 | tf_op jit(solution)/shard_map/all_gather | solution.py:108
  497.3 129.8 %all-gather.13.cloned.1.call-start = ((), (), s32[]{:S(2)}) async-start(), calls=%async_computation.11 | async-start | bytes 2506752 | tf_op jit(solution)/shard_map/all_gather | solution.py:109
  497.8 224.4 %all-reduce.10.cloned.1.call-start = ((), (), s32[]{:S(2)}) async-start(), calls=%async_computation.12 | async-start | bytes 6291456 | tf_op jit(solution)/shard_map/psum | solution.py:190
  529.0 193.3 %copy-start.37 = (f32[768]{0:T(1024)}, f32[768]{0:T(1024)S(1)}, u32[]{:S(2)}) copy-start(f32[768]{0:T(1024)S(1)} %get-tuple-element.637) | copy-start | bytes 9220
  558.4 173.0 %copy-start.29 = (f32[768]{0:T(1024)}, f32[768]{0:T(1024)S(1)}, u32[]{:S(2)}) copy-start(f32[768]{0:T(1024)S(1)} %get-tuple-element.639) | copy-start | bytes 9220
  558.4 298.5 %copy-start.33 = (f32[768]{0:T(1024)}, f32[768]{0:T(1024)S(1)}, u32[]{:S(2)}) copy-start(f32[768]{0:T(1024)S(1)} %get-tuple-element.640) | copy-start | bytes 9220
  636.3 211.2 %all-reduce.12.cloned.1.call-start = ((), (), s32[]{:S(2)}) async-start(), calls=%async_computation.13 | async-start | bytes 6291456 | tf_op jit(solution)/shard_map/psum | solution.py:206
  761.5 706.0 %reduce-scatter.12.cloned.1.call-start = ((), (), s32[]{:S(2)}) async-start(), calls=%async_computation.14 | async-start | bytes 7864320 | tf_op jit(solution)/shard_map/reduce_scatter | solution.py:253
  761.8 95.1 %copy-start.32 = (f32[2048]{0:T(1024)S(1)}, f32[2048]{0:T(1024)}, u32[]{:S(2)}) copy-start(f32[2048]{0:T(1024)} %copy-done.31) | copy-start | bytes 24580
  1356.5 224.6 %reduce-scatter.14.cloned.1.call-start = ((), (), s32[]{:S(2)}) async-start(), calls=%async_computation.15 | async-start | bytes 7864320 | tf_op jit(solution)/shard_map/reduce_scatter | solution.py:256
  1357.3 288.9 %reduce-scatter.22.cloned.1.call-start = ((), (), s32[]{:S(2)}) async-start(), calls=%async_computation.20 | async-start | bytes 417792
  1359.9 350.2 %reduce-scatter.24.cloned.1.call-start = ((), (), s32[]{:S(2)}) async-start(), calls=%async_computation.21 | async-start | bytes 417792
  1365.7 218.0 %copy-start.9 = (bf16[2,1024,768]{2,1,0:T(8,128)(2,1)S(1)}, bf16[2,1024,768]{2,1,0:T(8,128)(2,1)}, u32[]{:S(2)}) copy-start(bf16[2,1024,768]{2,1,0:T(8,128)(2,1)} %param.16) | copy-start | bytes 9437188
  1372.3 400.6 %all-reduce.16.cloned.1.call-start = ((), (), s32[]{:S(2)}) async-start(), calls=%async_computation.22 | async-start | bytes 9437184
  1598.3 208.1 %all-reduce.14.cloned.1.call-start = ((), (), s32[]{:S(2)}) async-start(), calls=%async_computation.16 | async-start | bytes 6291456 | tf_op jit(solution)/shard_map/psum | solution.py:276
  1607.5 204.4 %reduce-scatter.16.cloned.1.call-start = ((), (), s32[]{:S(2)}) async-start(), calls=%async_computation.17 | async-start | bytes 1253376 | tf_op jit(solution)/shard_map/reduce_scatter | solution.py:284
  1613.5 238.6 %reduce-scatter.20.cloned.1.call-start = ((), (), s32[]{:S(2)}) async-start(), calls=%async_computation.19 | async-start | bytes 5013504 | tf_op jit(solution)/shard_map/reduce_scatter | solution.py:286
  1624.2 307.0 %reduce-scatter.18.cloned.1.call-start = ((), (), s32[]{:S(2)}) async-start(), calls=%async_computation.18 | async-start | bytes 5013504 | tf_op jit(solution)/shard_map/reduce_scatter | solution.py:285
  1636.2 75.2 %copy-start.16 = (bf16[2,1024,384]{1,2,0:T(8,128)(2,1)S(1)}, bf16[2,1024,384]{1,2,0:T(8,128)(2,1)}, u32[]{:S(2)}) copy-start(bf16[2,1024,384]{1,2,0:T(8,128)(2,1)} %reduce-scatter.14.cloned.1.call-done) | copy-start | bytes 4718596
  1636.2 75.5 %copy-start.45 = (f32[1536]{0:T(1024)S(1)}, f32[1536]{0:T(1024)}, u32[]{:S(2)}) copy-start(f32[1536]{0:T(1024)} %get-tuple-element.708) | copy-start | bytes 18436
  (39 other events, 245.8 us)
Sparse Core Ops, SparseCore 0:
  84.1 124.1 all-gather.8
  210.5 114.2 all-gather.6
  496.8 84.8 all-reduce.7
  636.4 85.7 all-reduce.9
  761.6 85.8 all-reduce.11
  1356.7 110.7 reduce-scatter.11
  1469.8 111.2 reduce-scatter.13
  1584.6 61.5 reduce-scatter.21
  1649.7 60.3 reduce-scatter.23
  1714.1 58.8 reduce-scatter.15
  1777.5 74.5 reduce-scatter.19
  1856.4 74.7 reduce-scatter.17
Sparse Core Ops, SparseCore 1:
  499.5 41.4 all-gather.10
  543.1 40.7 all-gather.12
  1598.3 120.1 all-reduce.15
  1720.8 85.4 all-reduce.13
